TPU v7x, 32 devices: a whole 2x2x4 slice. The times are simulated.
32 devices in a mesh: row: 2 (over x), col: 4 (over z), grp: 4 (over y, core).
Axes of the slice: x: 2, y: 2, z: 4, core: 2. Of those that a mesh axis runs over, the one named last changes fastest.
Arguments:
- tokens: bfloat16 [8, 256, 2048], P(('grp', 'row'), None, 'col'), may hold values from -8 to 8
- w_query: bfloat16 [2048, 2048], P(None, 'col'), may hold values from -0.125 to 0.125
- w_key: bfloat16 [2048, 2048], P(None, 'col'), may hold values from -0.125 to 0.125
- w_value: bfloat16 [2048, 2048], P(None, 'col'), may hold values from -0.125 to 0.125
- w_out: bfloat16 [2048, 2048], P('col'), may hold values from -0.125 to 0.125
- diff_lambda: float32 [8], replicated, may hold values from 0.2 to 0.8
- prefix_keys: bfloat16 [8, 4, 256, 2048], P(('grp', 'row'), None, None, 'col'), may hold values from -800 to 800
- prefix_values: bfloat16 [8, 4, 256, 2048], P(('grp', 'row'), None, None, 'col'), may hold values from -6 to 6
- new_len: int32 [8], P(('grp', 'row')), may hold values from 64 to 256
- prefix_len: int32 [8], P(('grp', 'row')), may hold values from 0 to 1024, as said below
- holder: int32 [8, 4], P(('grp', 'row')), may hold values from 0 to 3, as said below
- page_table: int32 [8, 4], replicated, may hold values from 0 to 3, as said below
Outputs:
- hidden: bfloat16 [8, 256, 2048], P(('grp', 'row'), None, 'col')
- page_keys: bfloat16 [4, 2, 4, 64, 2048], P('grp', 'row', None, None, 'col')
- page_values: bfloat16 [4, 2, 4, 64, 2048], P('grp', 'row', None, None, 'col')
Inputs may be any that keep to these rules, and one draw needn't show every extreme that they name: `prefix_len`: half of the requests have no prefix; one has exactly 1024. Each row of holder names every group once. For each r and b, the entries page_table[g * 2 + r, b] over the 4 groups g name every slot once.
All inputs are finite; a program needn't handle non-finite values.
Results may differ from a plain program's by a relative error of at most 0.0078.
Values may be sent and summed in bfloat16 or wider, within the bound.
A program may use at most 64 MiB of HBM per device.

v0:
```python
import jax
import jax.numpy as jnp
from jax import lax
from jax.sharding import PartitionSpec as P

D = 2048
DK = 128
DV = 256


EPS_INPUT = 1e-06
EPS_HEAD = 1e-05
OUT_SCALE = 0.8


def swapped(x, axis, stride):
    return lax.ppermute(x, axis, [(i, i ^ 1 << stride) for i in range(lax.axis_size(axis))])


def head_attend(queries_in, key_set, value_set, allowed):
    scores = jnp.einsum(
        "chd,khd->hck", queries_in, key_set, preferred_element_type=jnp.float32
    ) * queries_in.shape[-1] ** (-0.5)
    scores = jnp.where(allowed[None], scores, -jnp.inf)
    highest = jnp.max(scores, axis=-1, keepdims=True)
    exp_scores = jnp.exp(scores - highest)
    weights = (exp_scores / jnp.sum(exp_scores, axis=-1, keepdims=True)).astype(jnp.bfloat16)
    return jnp.einsum("hck,khe->che", weights, value_set, preferred_element_type=jnp.float32)


def arrange(is_first, own_part, other_part):
    return (jnp.where(is_first, own_part, other_part), jnp.where(is_first, other_part, own_part))


def head_norm(differ):
    return (
        OUT_SCALE * differ * lax.rsqrt(jnp.mean(differ * differ, axis=-1, keepdims=True) + EPS_HEAD)
    )


def local(
    tokens,
    w_query,
    w_key,
    w_value,
    w_out,
    diff_lambda,
    prefix_keys,
    prefix_values,
    new_len,
    prefix_len,
    holder,
    page_table,
):
    groups = lax.axis_size("grp")
    row_count = lax.axis_size("row")
    grp_index = lax.axis_index("grp")
    row_index = lax.axis_index("row")
    col_index = lax.axis_index("col")
    local_tokens = tokens[0]
    slot_count = local_tokens.shape[0]
    query_cols = w_query.shape[1]
    value_cols = w_value.shape[1]
    group_ids = jnp.arange(groups, dtype=jnp.int32)
    got_keys, got_values = (
        lax.all_to_all(prefix_keys[0], "grp", split_axis=0, concat_axis=0, tiled=True),
        lax.all_to_all(prefix_values[0], "grp", split_axis=0, concat_axis=0, tiled=True),
    )
    shard_piece = lax.all_gather(local_tokens, "col", axis=1, tiled=True)

    def partial_product(weight):
        return jnp.dot(shard_piece, weight, preferred_element_type=jnp.float32)

    as_float = shard_piece.astype(jnp.float32)
    query_sum = partial_product(w_query)
    key_sum = partial_product(w_key)
    value_sum = partial_product(w_value)
    square_sum = jnp.sum(as_float * as_float, axis=1)
    inv_rms = lax.rsqrt(square_sum / D + EPS_INPUT)[:, None]
    queries = (query_sum * inv_rms).astype(jnp.bfloat16)
    new_keys = (key_sum * inv_rms).astype(jnp.bfloat16)
    new_values = (value_sum * inv_rms).astype(jnp.bfloat16)
    is_live = jnp.arange(slot_count) < new_len[0]
    zero_entry = jnp.zeros((), jnp.bfloat16)
    page_size = slot_count // groups
    send_keys = jnp.where(is_live[:, None], new_keys, zero_entry).reshape(
        groups, page_size, query_cols
    )
    send_values = jnp.where(is_live[:, None], new_values, zero_entry).reshape(
        groups, page_size, value_cols
    )
    recv_keys, recv_values = (
        lax.all_to_all(send_keys, "grp", split_axis=0, concat_axis=0, tiled=True),
        lax.all_to_all(send_values, "grp", split_axis=0, concat_axis=0, tiled=True),
    )
    pick_block = (holder[0][:, None] == group_ids[None, :]).astype(jnp.bfloat16)
    fetched_keys = (
        jnp.einsum("bh,hpc->bpc", pick_block, got_keys, preferred_element_type=jnp.float32)
        .astype(jnp.bfloat16)
        .reshape(-1, query_cols)
    )
    fetched_values = (
        jnp.einsum("bh,hpc->bpc", pick_block, got_values, preferred_element_type=jnp.float32)
        .astype(jnp.bfloat16)
        .reshape(-1, value_cols)
    )
    prefix_span = fetched_keys.shape[0]
    position = jnp.arange(prefix_span + slot_count)
    within = jnp.arange(slot_count)
    allowed = jnp.where(
        position[None, :] < prefix_span,
        position[None, :] < prefix_len[0],
        position[None, :] - prefix_span <= within[:, None],
    )
    key_own = jnp.concatenate([fetched_keys, new_keys], axis=0)
    value_own = jnp.concatenate([fetched_values, new_values], axis=0)
    if query_cols == DK:
        is_first = col_index % 2 == 0
        head_lam = diff_lambda[col_index // 2]
        half_width = DV // 2
        partner_query, partner_key, partner_value, partner_pkey, partner_pvalue = swapped(
            (queries, new_keys, new_values, fetched_keys, fetched_values), "col", 0
        )
        query_zero, query_one = arrange(is_first, queries, partner_query)
        key_zero, key_one = arrange(
            is_first, key_own, jnp.concatenate([partner_pkey, partner_key], axis=0)
        )
        value_low, value_high = arrange(
            is_first, value_own, jnp.concatenate([partner_pvalue, partner_value], axis=0)
        )
        value_full = jnp.concatenate([value_low, value_high], axis=1)[:, None, :]
        map_zero = head_attend(query_zero[:, None, :], key_zero[:, None, :], value_full, allowed)
        map_one = head_attend(query_one[:, None, :], key_one[:, None, :], value_full, allowed)
        normed = head_norm(map_zero - head_lam * map_one)
        attended = lax.dynamic_slice_in_dim(
            normed[:, 0, :], col_index % 2 * half_width, half_width, 1
        ).astype(jnp.bfloat16)
    else:
        local_heads = query_cols // (2 * DK)
        query_four = queries.reshape(slot_count, local_heads, 2, DK)
        key_four = key_own.reshape(-1, local_heads, 2, DK)
        value_three = value_own.reshape(-1, local_heads, DV)
        map_zero = head_attend(query_four[:, :, 0], key_four[:, :, 0], value_three, allowed)
        map_one = head_attend(query_four[:, :, 1], key_four[:, :, 1], value_three, allowed)
        head_lam = lax.dynamic_slice_in_dim(diff_lambda, col_index * local_heads, local_heads, 0)
        normed = head_norm(map_zero - head_lam[None, :, None] * map_one)
        attended = normed.reshape(slot_count, local_heads * DV).astype(jnp.bfloat16)
    mixed = lax.psum_scatter(
        lax.dot_general(
            w_out, attended, (((0,), (1,)), ((), ())), preferred_element_type=jnp.float32
        ),
        "col",
        scatter_dimension=0,
        tiled=True,
    ).T
    combined = local_tokens.astype(jnp.float32) + mixed
    hidden = jnp.where(is_live[:, None], combined, 0.0).astype(jnp.bfloat16)[None]
    sources = group_ids * row_count + row_index
    slot_of = page_table[sources, grp_index]
    placement_map = (slot_of[None, :] == group_ids[:, None]).astype(jnp.bfloat16)
    page_keys = jnp.einsum(
        "sg,gpc->spc", placement_map, recv_keys, preferred_element_type=jnp.float32
    ).astype(jnp.bfloat16)[None, None]
    page_values = jnp.einsum(
        "sg,gpc->spc", placement_map, recv_values, preferred_element_type=jnp.float32
    ).astype(jnp.bfloat16)[None, None]
    return (hidden, page_keys, page_values)


def solution(mesh):
    placed = (
        P(("grp", "row"), None, "col"),
        P(None, "col"),
        P(None, "col"),
        P(None, "col"),
        P("col", None),
        P(),
        P(("grp", "row"), None, None, "col"),
        P(("grp", "row"), None, None, "col"),
        P(("grp", "row")),
        P(("grp", "row")),
        P(("grp", "row"), None),
        P(),
    )
    return jax.shard_map(
        local,
        mesh=mesh,
        in_specs=placed,
        out_specs=(
            P(("grp", "row"), None, "col"),
            P("grp", "row", None, None, "col"),
            P("grp", "row", None, None, "col"),
        ),
        check_vma=False,
    )
```

profile of v0, /device:TPU:0, one launch (start us, length us, event | category | flops | bytes accessed | tf_op | source)
XLA Modules:
  0.0 138.5 jit_solution(12786974933693817800)
XLA Ops:
  7.2 4.4 %all-to-all-start.1 = ((bf16[4,256,512]{2,1,0:T(8,128)(2,1)}), bf16[4,256,512]{2,1,0:T(8,128)(2,1)S(1)}, u32[]{:S(2)}, u32[]{:S(2)}) async-start(bf16[4,256,512]{2,1,0:T(8,128)(2,1)} %bitcast.92), calls=%async_computation.1 | async-start | bytes 2097152 | tf_op jit(solution)/shard_map/all_to_all | solution.py:66
  13.6 12.4 %all-to-all-done.1 = bf16[4,256,512]{2,1,0:T(8,128)(2,1)S(1)} async-done(((bf16[4,256,512]{2,1,0:T(8,128)(2,1)}), bf16[4,256,512]{2,1,0:T(8,128)(2,1)S(1)}, u32[]{:S(2)}, u32[]{:S(2)}) %all-to-all-start.1) | async-done | bytes 1048608 | tf_op jit(solution)/shard_map/all_to_all | solution.py:66
  26.0 4.3 %all-to-all-start = ((bf16[4,256,512]{2,1,0:T(8,128)(2,1)}), bf16[4,256,512]{2,1,0:T(8,128)(2,1)}, u32[]{:S(2)}, u32[]{:S(2)}) async-start(bf16[4,256,512]{2,1,0:T(8,128)(2,1)} %bitcast.4), calls=%async_computation | async-start | bytes 2097152 | tf_op jit(solution)/shard_map/all_to_all | solution.py:67
  32.4 1.2 copy.45
  33.6 1.3 concatenate.22
  34.9 9.9 %all-to-all-done = bf16[4,256,512]{2,1,0:T(8,128)(2,1)} async-done(((bf16[4,256,512]{2,1,0:T(8,128)(2,1)}), bf16[4,256,512]{2,1,0:T(8,128)(2,1)}, u32[]{:S(2)}, u32[]{:S(2)}) %all-to-all-start) | async-done | bytes 1048608 | tf_op jit(solution)/shard_map/all_to_all | solution.py:67
  44.8 3.2 %convolution_convert_fusion.1 = bf16[4,256,512]{2,0,1:T(4,128)(2,1)} fusion(bf16[4,256,512]{2,1,0:T(8,128)(2,1)} %all-to-all-done, s32[4]{0:T(128)S(1)} %bitcast.96), kind=kOutput, calls=%fused_computation.16 | convolution fusion | flops 4718608 | bytes 2097168 | tf_op jit(solution)/shard_map/bh,hpc->bpc/dot_general | solution.py:103
  48.0 3.8 %copy.53 = bf16[4,256,512]{1,0,2:T(4,128)(2,1)} copy(bf16[4,256,512]{2,0,1:T(4,128)(2,1)} %convolution_convert_fusion.1) | data formatting | bytes 2097152 | tf_op jit(solution)/shard_map/concatenate | solution.py:116
  51.8 2.6 %reshape.147 = bf16[1024,2,256]{0,2,1:T(8,128)(2,1)} reshape(bf16[4,256,512]{1,0,2:T(4,128)(2,1)} %copy.53) | data formatting | bytes 2097152 | tf_op jit(solution)/shard_map/concatenate | solution.py:116
  55.5 1.5 %multiply_reduce_fusion = f32[256]{0:T(256)S(1)} fusion(bf16[1,256,2048]{2,1,0:T(8,128)(2,1)} %all-gather.3.cloned.1.call-done), kind=kLoop, calls=%fused_computation.14 | loop fusion | flops 1572608 | bytes 1049600 | tf_op jit(solution)/shard_map/reduce_sum | solution.py:78
  57.1 2.7 %fusion.16 = bf16[256,512]{1,0:T(8,128)(2,1)S(1)} fusion(bf16[2048,512]{1,0:T(8,128)(2,1)} %param.14, bf16[1,256,2048]{2,1,0:T(8,128)(2,1)} %all-gather.3.cloned.1.call-done, f32[256]{0:T(256)S(1)} %add_rsqrt_fusion), kind=kOutput, calls=%fused_computation.30 | convolution fusion | flops 537133056 | bytes 3408896 | tf_op jit(solution)/shard_map/dot_general | solution.py:72
  60.6 3.0 %fusion.15 = bf16[256,512]{1,0:T(8,128)(2,1)} fusion(bf16[2048,512]{1,0:T(8,128)(2,1)} %param.13, bf16[1,256,2048]{2,1,0:T(8,128)(2,1)S(1)} %copy-done.2, f32[256]{0:T(256)S(1)} %add_rsqrt_fusion), kind=kOutput, calls=%fused_computation.29 | convolution fusion | flops 537133056 | bytes 3408896 | tf_op jit(solution)/shard_map/dot_general | solution.py:72
  65.7 3.2 %broadcast_select_fusion = (bf16[256,512]{1,0:T(8,128)(2,1)}, bf16[256,512]{1,0:T(8,128)(2,1)}, bf16[256,512]{1,0:T(8,128)(2,1)}) fusion(pred[256]{0:T(512)(128)(4,1)S(1)} %iota_compare_fusion.5, bf16[256,512]{1,0:T(8,128)(2,1)} %copy-done.8, f32[256]{0:T(256)S(1)} %add_rsqrt_fusion, bf16[2048,512]{1,0:T(8,128)(2,1)} %param.15, ...), kind=kOutput, calls=%fused_computation.52 | convolution fusion | flops 537395200 | bytes 4195584 | tf_op jit(solution)/shard_map/dot_general | solution.py:72
  69.0 1.8 %copy.54 = bf16[256,512]{0,1:T(8,128)(2,1)} copy(bf16[256,512]{1,0:T(8,128)(2,1)} %get-tuple-element.22) | data formatting | bytes 524288 | tf_op jit(solution)/shard_map/concatenate | solution.py:116
  71.5 3.9 %fusion.52 = (f32[2,256]{1,0:T(2,128)S(1)}, f32[2,256,1280]{2,1,0:T(8,128)}) fusion(pred[256,1280]{1,0:T(8,128)(4,1)} %fusion.10, bf16[1280,2,2,128]{3,0,1,2:T(8,128)(2,1)} %copy_dynamic-update-slice_fusion.1, bf16[256,2,1,128]{3,2,1,0:T(2,128)(2,1)} %get-tuple-element.13), kind=kOutput, calls=%fused_computation.84 | convolution fusion | flops 170394880 | bytes 3868672 | tf_op jit(solution)/shard_map/sub | solution.py:26
  75.4 3.8 %fusion.53 = (f32[2,256]{1,0:T(2,128)S(1)}, f32[2,256,1280]{2,1,0:T(8,128)}) fusion(pred[256,1280]{1,0:T(8,128)(4,1)S(1)} %copy-done.6, bf16[1280,2,2,128]{3,0,1,2:T(8,128)(2,1)} %copy_dynamic-update-slice_fusion.1, bf16[256,2,1,128]{3,2,1,0:T(2,128)(2,1)} %get-tuple-element.12), kind=kOutput, calls=%fused_computation.85 | convolution fusion | flops 170394880 | bytes 3868672 | tf_op jit(solution)/shard_map/sub | solution.py:26
  79.2 2.6 %fusion.8 = f32[2,256,256]{2,1,0:T(8,128)S(1)} fusion(f32[2,256,1280]{2,1,0:T(8,128)} %get-tuple-element.17, f32[2,256]{1,0:T(2,128)S(1)} %get-tuple-element.16, bf16[256,2,256]{0,2,1:T(8,128)(2,1)} %bitcast.93, bf16[1024,2,256]{0,2,1:T(8,128)(2,1)S(1)} %copy-done.3), kind=kOutput, calls=%fused_computation.19 | convolution fusion | flops 339476480 | bytes 4458496 | tf_op jit(solution)/shard_map/hck,khe->che/dot_general | solution.py:28
  82.7 2.1 %convolution_bitcast_fusion = f32[2048,256]{0,1:T(8,128)} fusion(bf16[256,512]{0,1:T(8,128)(2,1)S(1)} %bitcast.91, bf16[512,2048]{1,0:T(8,128)(2,1)S(1)} %copy-done), kind=kOutput, calls=%fused_computation.11 | convolution fusion | flops 536870912 | bytes 4456448 | tf_op jit(solution)/shard_map/dot_general | solution.py:149
  84.8 3.5 %all-to-all-start.2 = ((bf16[4,64,512]{2,1,0:T(8,128)(2,1)}), bf16[4,64,512]{2,1,0:T(8,128)(2,1)S(1)}, u32[]{:S(2)}, u32[]{:S(2)}) async-start(bf16[4,64,512]{2,1,0:T(8,128)(2,1)} %bitcast.20), calls=%async_computation.3 | async-start | bytes 524288 | tf_op jit(solution)/shard_map/all_to_all | solution.py:93
  88.4 6.0 %all-to-all-done.2 = bf16[4,64,512]{2,1,0:T(8,128)(2,1)S(1)} async-done(((bf16[4,64,512]{2,1,0:T(8,128)(2,1)}), bf16[4,64,512]{2,1,0:T(8,128)(2,1)S(1)}, u32[]{:S(2)}, u32[]{:S(2)}) %all-to-all-start.2) | async-done | bytes 262176 | tf_op jit(solution)/shard_map/all_to_all | solution.py:93
  94.4 3.4 %all-to-all-start.3 = ((bf16[4,64,512]{2,1,0:T(8,128)(2,1)}), bf16[4,64,512]{2,1,0:T(8,128)(2,1)S(1)}, u32[]{:S(2)}, u32[]{:S(2)}) async-start(bf16[4,64,512]{2,1,0:T(8,128)(2,1)} %bitcast.22), calls=%async_computation.4 | async-start | bytes 524288 | tf_op jit(solution)/shard_map/all_to_all | solution.py:94
  99.5 4.3 %all-to-all-done.3 = bf16[4,64,512]{2,1,0:T(8,128)(2,1)S(1)} async-done(((bf16[4,64,512]{2,1,0:T(8,128)(2,1)}), bf16[4,64,512]{2,1,0:T(8,128)(2,1)S(1)}, u32[]{:S(2)}, u32[]{:S(2)}) %all-to-all-start.3) | async-done | bytes 262176 | tf_op jit(solution)/shard_map/all_to_all | solution.py:94
  104.8 25.0 %reduce-scatter.2.cloned.1.call-done = f32[512,256]{0,1:T(8,128)} async-done(((f32[2048,256]{0,1:T(8,128)}), f32[512,256]{0,1:T(8,128)}) %reduce-scatter.2.cloned.1.call-update) | async-done | bytes 524304 | tf_op jit(solution)/shard_map/reduce_scatter | solution.py:148
  129.8 1.9 %fusion.26 = bf16[1,256,512]{2,1,0:T(8,128)(2,1)} fusion(f32[512,256]{0,1:T(8,128)} %reduce-scatter.2.cloned.1.call-done, bf16[1,256,512]{2,1,0:T(8,128)(2,1)S(1)} %copy-done.5, pred[256]{0:T(512)(128)(4,1)S(1)} %iota_compare_fusion.5), kind=kLoop, calls=%fused_computation.48 | loop fusion | flops 524288 | bytes 1048832 | tf_op jit(solution)/shard_map/broadcast_in_dim | solution.py:157
  (50 shorter events, 11.2 us)
Async XLA Ops:
  7.2 75.5 %copy-start = (bf16[512,2048]{1,0:T(8,128)(2,1)S(1)}, bf16[512,2048]{1,0:T(8,128)(2,1)}, u32[]{:S(2)}) copy-start(bf16[512,2048]{1,0:T(8,128)(2,1)} %param.16) | copy-start | bytes 6291460
  7.2 23.2 %copy-start.9 = (f32[8]{0:T(128)S(1)}, f32[8]{0:T(128)}, u32[]{:S(2)}) copy-start(f32[8]{0:T(128)} %param.17) | copy-start | bytes 100
  7.2 24.2 %copy-start.10 = (s32[1,4]{1,0:T(1,128)S(1)}, s32[1,4]{1,0:T(1,128)}, u32[]{:S(2)}) copy-start(s32[1,4]{1,0:T(1,128)} %param.22) | copy-start | bytes 52
  7.2 18.8 %all-to-all-start.1 = ((bf16[4,256,512]{2,1,0:T(8,128)(2,1)}), bf16[4,256,512]{2,1,0:T(8,128)(2,1)S(1)}, u32[]{:S(2)}, u32[]{:S(2)}) async-start(bf16[4,256,512]{2,1,0:T(8,128)(2,1)} %bitcast.92), calls=%async_computation.1 | async-start | bytes 2097152 | tf_op jit(solution)/shard_map/all_to_all | solution.py:66
  11.6 44.0 %all-gather.3.cloned.1.call-start = ((), (), s32[]{:S(2)}) async-start(), calls=%async_computation.6 | async-start | bytes 1310720 | tf_op jit(solution)/shard_map/all_gather | solution.py:69
  26.0 18.8 %all-to-all-start = ((bf16[4,256,512]{2,1,0:T(8,128)(2,1)}), bf16[4,256,512]{2,1,0:T(8,128)(2,1)}, u32[]{:S(2)}, u32[]{:S(2)}) async-start(bf16[4,256,512]{2,1,0:T(8,128)(2,1)} %bitcast.4), calls=%async_computation | async-start | bytes 2097152 | tf_op jit(solution)/shard_map/all_to_all | solution.py:67
  30.3 99.5 %reduce-scatter.2.cloned.1.call-start = ((), (), s32[]{:S(2)}) async-start(), calls=%async_computation.5 | async-start | bytes 2621440 | tf_op jit(solution)/shard_map/reduce_scatter | solution.py:148
  57.1 3.5 %copy-start.2 = (bf16[1,256,2048]{2,1,0:T(8,128)(2,1)S(1)}, bf16[1,256,2048]{2,1,0:T(8,128)(2,1)}, u32[]{:S(2)}) copy-start(bf16[1,256,2048]{2,1,0:T(8,128)(2,1)} %all-gather.3.cloned.1.call-done) | copy-start | bytes 3145732
  59.8 0.8 copy-start.8
  65.7 5.1 %copy-start.4 = (bf16[256,2,2,128]{3,2,1,0:T(2,128)(2,1)S(1)}, bf16[256,2,2,128]{3,2,1,0:T(2,128)(2,1)}, u32[]{:S(2)}) copy-start(bf16[256,2,2,128]{3,2,1,0:T(2,128)(2,1)} %concatenate.23) | copy-start | bytes 786436
  71.5 3.9 %copy-start.6 = (pred[256,1280]{1,0:T(8,128)(4,1)S(1)}, pred[256,1280]{1,0:T(8,128)(4,1)}, u32[]{:S(2)}) copy-start(pred[256,1280]{1,0:T(8,128)(4,1)} %fusion.10) | copy-start | bytes 983044
  75.4 3.8 %copy-start.3 = (bf16[1024,2,256]{0,2,1:T(8,128)(2,1)S(1)}, bf16[1024,2,256]{0,2,1:T(8,128)(2,1)}, u32[]{:S(2)}) copy-start(bf16[1024,2,256]{0,2,1:T(8,128)(2,1)} %reshape.147) | copy-start | bytes 3145732
  79.2 2.6 %copy-start.7 = (bf16[256,512]{0,1:T(8,128)(2,1)S(1)}, bf16[256,512]{0,1:T(8,128)(2,1)}, u32[]{:S(2)}) copy-start(bf16[256,512]{0,1:T(8,128)(2,1)} %copy.54) | copy-start | bytes 786436
  79.2 2.7 %copy-start.11 = (f32[2,256,1280]{2,1,0:T(8,128)S(1)}, f32[2,256,1280]{2,1,0:T(8,128)}, u32[]{:S(2)}) copy-start(f32[2,256,1280]{2,1,0:T(8,128)} %get-tuple-element.19) | copy-start | bytes 7864324
  84.8 13.0 %copy-start.1 = (s32[8,4]{0,1:T(4,128)S(1)}, s32[8,4]{0,1:T(4,128)}, u32[]{:S(2)}) copy-start(s32[8,4]{0,1:T(4,128)} %param.23) | copy-start | bytes 388
  84.8 45.0 %copy-start.5 = (bf16[1,256,512]{2,1,0:T(8,128)(2,1)S(1)}, bf16[1,256,512]{2,1,0:T(8,128)(2,1)}, u32[]{:S(2)}) copy-start(bf16[1,256,512]{2,1,0:T(8,128)(2,1)} %param.12) | copy-start | bytes 786436
  84.8 9.6 %all-to-all-start.2 = ((bf16[4,64,512]{2,1,0:T(8,128)(2,1)}), bf16[4,64,512]{2,1,0:T(8,128)(2,1)S(1)}, u32[]{:S(2)}, u32[]{:S(2)}) async-start(bf16[4,64,512]{2,1,0:T(8,128)(2,1)} %bitcast.20), calls=%async_computation.3 | async-start | bytes 524288 | tf_op jit(solution)/shard_map/all_to_all | solution.py:93
  94.4 9.4 %all-to-all-start.3 = ((bf16[4,64,512]{2,1,0:T(8,128)(2,1)}), bf16[4,64,512]{2,1,0:T(8,128)(2,1)S(1)}, u32[]{:S(2)}, u32[]{:S(2)}) async-start(bf16[4,64,512]{2,1,0:T(8,128)(2,1)} %bitcast.22), calls=%async_computation.4 | async-start | bytes 524288 | tf_op jit(solution)/shard_map/all_to_all | solution.py:94
Sparse Core Ops, SparseCore 0:
  14.0 30.3 all-gather.2
  84.9 44.8 reduce-scatter.1
where the time goes:
time: 139 us
  waiting for transfers between devices  58.3 us (42%)
  matrix products  26.6 us (19%)
  local copies, waits for them, and re-layouts  17.9 us (13%)
  starting transfers between devices  15.6 us (11%)
  between operations  15.6 us (11%)
  other arithmetic  4.4 us (3%)
    reduce_scatter x1, waiting for transfers between devices, local(): lax.psum_scatter(lax.dot_general(w_out, attended, (((0,), (1,)), ((), ())...  25 us
    all_to_all x1, waiting for transfers between devices, local(): lax.all_to_all(prefix_keys[0], 'grp', split_axis=0, concat_axis=0, tiled=...  12.4 us
    all_to_all x1, waiting for transfers between devices, local(): lax.all_to_all(prefix_values[0], 'grp', split_axis=0, concat_axis=0, tile...  9.92 us
    dot_general x3, matrix products, partial_product(): return jnp.dot(shard_piece, weight, preferred_element_type=jnp.float32)  8.92 us
    concatenate x3, local copies, waits for them, and re-layouts, local(): value_own = jnp.concatenate([fetched_values, new_values], axis=0)  8.22 us
    sub x2, matrix products, head_attend(): exp_scores = jnp.exp(scores - highest)  7.68 us
    all_to_all x1, waiting for transfers between devices, local(): lax.all_to_all(send_keys, 'grp', split_axis=0, concat_axis=0, tiled=True)  6 us
    all_to_all x1, starting transfers between devices, local(): lax.all_to_all(prefix_keys[0], 'grp', split_axis=0, concat_axis=0, tiled=...  4.38 us
  transfers between devices with their start and end apart: 6, of which 5 were waited for; matrix products, arithmetic and copies ran while one was open for 13% of the time, Pallas kernels for 0%

commit v1 on v0

--- a/solution.py
+++ b/solution.py
@@ -1,6 +1,9 @@
+import functools
 import jax
 import jax.numpy as jnp
 from jax import lax
+from jax.experimental import pallas as pl
+from jax.experimental.pallas import tpu as pltpu
 from jax.sharding import PartitionSpec as P
 
 D = 2048
@@ -35,6 +38,336 @@
 def head_norm(differ):
     return (
         OUT_SCALE * differ * lax.rsqrt(jnp.mean(differ * differ, axis=-1, keepdims=True) + EPS_HEAD)
+    )
+
+
+MASKED = -1e30
+LOG2E = 1.4426950408889634
+
+
+def fits_kernel(w_query, prefix_keys):
+    return w_query.shape[1] % (2 * DK) == 0 and lax.axis_size("grp") == 4
+
+
+def kernel(
+    n_col,
+    n_row,
+    new_len,
+    prefix_len,
+    holder,
+    page_table,
+    diff_lambda,
+    tokens,
+    w_query,
+    w_key,
+    w_value,
+    w_out,
+    prefix_keys,
+    prefix_values,
+    hidden,
+    page_keys,
+    page_values,
+    tok,
+    weights,
+    w_last,
+    kbuf,
+    vbuf,
+    sums,
+    queries,
+    acc,
+    top,
+    low,
+    attended,
+    outgoing,
+    incoming,
+    page_out,
+    page_in,
+    local_sem,
+    tok_send,
+    tok_recv,
+    pre_send,
+    pre_recv,
+    page_send,
+    page_recv,
+    mix_send,
+    mix_recv,
+):
+    groups = 4
+    grp = lax.axis_index("grp")
+    row = lax.axis_index("row")
+    col = lax.axis_index("col")
+    slots, cols = tok.shape[1], tok.shape[2]
+    heads = queries.shape[1] // (2 * DK)
+    block = kbuf.shape[1]
+    page = slots // groups
+    peers = (None, grp + 1 - 2 * lax.rem(grp, 2), lax.rem(grp + 2, groups), groups - 1 - grp)
+
+    def ahead(step):
+        return lax.rem(col + step, n_col)
+
+    def behind(step):
+        return lax.rem(col + n_col - step, n_col)
+
+    copies = [
+        pltpu.make_async_copy(tokens.at[0], tok.at[0], local_sem.at[0]),
+        pltpu.make_async_copy(w_query, weights.at[0], local_sem.at[1]),
+        pltpu.make_async_copy(w_key, weights.at[1], local_sem.at[2]),
+        pltpu.make_async_copy(w_value, weights.at[2], local_sem.at[3]),
+        pltpu.make_async_copy(prefix_keys.at[0, grp], kbuf.at[0], local_sem.at[4]),
+        pltpu.make_async_copy(prefix_values.at[0, grp], vbuf.at[0], local_sem.at[5]),
+        pltpu.make_async_copy(w_out, w_last, local_sem.at[6]),
+    ]
+    barrier = pltpu.get_barrier_semaphore()
+    for step in range(1, n_col):
+        pl.semaphore_signal(
+            barrier, inc=1, device_id={"col": ahead(step)}, device_id_type=pl.DeviceIdType.MESH
+        )
+    for step in range(1, groups):
+        pl.semaphore_signal(
+            barrier, inc=1, device_id={"grp": peers[step]}, device_id_type=pl.DeviceIdType.MESH
+        )
+    for copy in copies:
+        copy.start()
+    pl.semaphore_wait(barrier, n_col - 1 + groups - 1)
+
+    def remote(source, target, send, recv, where):
+        return pltpu.make_async_remote_copy(
+            src_ref=source,
+            dst_ref=target,
+            send_sem=send,
+            recv_sem=recv,
+            device_id=where,
+            device_id_type=pl.DeviceIdType.MESH,
+        )
+
+    token_copies = [None] + [
+        remote(tokens.at[0], tok.at[step], tok_send.at[step], tok_recv.at[step], {"col": ahead(step)})
+        for step in range(1, n_col)
+    ]
+    for step in range(1, n_col):
+        token_copies[step].start()
+    key_copies, value_copies = [None], [None]
+    for step in range(1, groups):
+        peer = peers[step]
+        key_copies.append(
+            remote(
+                prefix_keys.at[0, peer], kbuf.at[step], pre_send.at[0, step], pre_recv.at[0, step], {"grp": peer}
+            )
+        )
+        value_copies.append(
+            remote(
+                prefix_values.at[0, peer], vbuf.at[step], pre_send.at[1, step], pre_recv.at[1, step], {"grp": peer}
+            )
+        )
+    for step in (2, 3, 1):
+        key_copies[step].start()
+        value_copies[step].start()
+
+    for copy in copies[:4]:
+        copy.wait()
+    square = jnp.zeros((slots, 1), jnp.float32)
+    for step in range(n_col):
+        if step:
+            token_copies[step].wait_recv()
+        shard = tok[step]
+        as_float = shard.astype(jnp.float32)
+        square = square + jnp.sum(as_float * as_float, axis=1, keepdims=True)
+        first = pl.multiple_of(behind(step) * cols, cols)
+        for which in range(3):
+            part = jnp.dot(
+                shard, weights[which, pl.ds(first, cols), :], preferred_element_type=jnp.float32
+            )
+            if step:
+                part = part + sums[which]
+            sums[which] = part
+    inv_rms = lax.rsqrt(square / D + EPS_INPUT)
+    live = lax.broadcasted_iota(jnp.int32, (slots, 1), 0) < new_len[0]
+    queries[...] = (sums[0] * inv_rms).astype(jnp.bfloat16)
+    new_keys = (sums[1] * inv_rms).astype(jnp.bfloat16)
+    new_values = (sums[2] * inv_rms).astype(jnp.bfloat16)
+    kbuf[groups] = new_keys
+    vbuf[groups] = new_values
+    page_out[0] = jnp.where(live, new_keys, jnp.zeros_like(new_keys))
+    page_out[1] = jnp.where(live, new_values, jnp.zeros_like(new_values))
+
+    scale = DK**-0.5 * LOG2E
+    key_at = lax.broadcasted_iota(jnp.int32, (slots, block), 1)
+    query_at = lax.broadcasted_iota(jnp.int32, (slots, block), 0)
+
+    def attend(index, allowed, first):
+        def one_head(head):
+            value = vbuf[index, :, head * DV : (head + 1) * DV]
+            for which in range(2):
+                at = head * 2 + which
+                scores = lax.dot_general(
+                    queries[:, at * DK : (at + 1) * DK],
+                    kbuf[index, :, at * DK : (at + 1) * DK],
+                    (((1,), (1,)), ((), ())),
+                    preferred_element_type=jnp.float32,
+                )
+                scores = jnp.where(allowed, scores * scale, MASKED)
+                highest = jnp.max(scores, axis=1, keepdims=True)
+                if not first:
+                    before = top[at]
+                    highest = jnp.maximum(before, highest)
+                weight = jnp.exp2(scores - highest)
+                total = jnp.sum(weight, axis=1, keepdims=True)
+                mixed = jnp.dot(weight.astype(jnp.bfloat16), value, preferred_element_type=jnp.float32)
+                if not first:
+                    decay = jnp.exp2(before - highest)
+                    total = total + low[at] * decay
+                    mixed = mixed + acc[at] * decay
+                top[at] = highest
+                low[at] = total
+                acc[at] = mixed
+
+        for head in range(heads):
+            one_head(head)
+
+    attend(groups, key_at <= query_at, True)
+    for step in range(groups):
+        if step:
+            key_copies[step].wait_recv()
+            value_copies[step].wait_recv()
+        else:
+            copies[4].wait()
+            copies[5].wait()
+        source = peers[step] if step else grp
+        place = jnp.int32(0)
+        for at in range(groups):
+            place = jnp.where(holder[0, at] == source, at, place)
+        attend(step, key_at < prefix_len[0] - place * block, False)
+
+    for head in range(heads):
+        zero, one = 2 * head, 2 * head + 1
+        differ = acc[zero] / low[zero] - diff_lambda[col * heads + head] * (acc[one] / low[one])
+        normed = OUT_SCALE * differ * lax.rsqrt(jnp.mean(differ * differ, axis=1, keepdims=True) + EPS_HEAD)
+        attended[:, head * DV : (head + 1) * DV] = normed.astype(jnp.bfloat16)
+
+    copies[6].wait()
+
+    def share(step):
+        first = pl.multiple_of(ahead(step) * cols, cols)
+        return jnp.dot(attended[...], w_last[:, pl.ds(first, cols)], preferred_element_type=jnp.float32)
+
+    mix_copies = [None]
+    for step in range(1, n_col):
+        outgoing[step] = share(step).astype(jnp.bfloat16)
+        copy = remote(
+            outgoing.at[step], incoming.at[step], mix_send.at[step], mix_recv.at[step], {"col": ahead(step)}
+        )
+        copy.start()
+        mix_copies.append(copy)
+
+    page_copies = []
+    for step in range(1, groups):
+        peer = peers[step]
+        rows = pl.ds(pl.multiple_of(peer * page, page), page)
+        for kind in range(2):
+            copy = remote(
+                page_out.at[kind, rows],
+                page_in.at[kind, grp],
+                page_send.at[kind, step],
+                page_recv.at[kind, step],
+                {"grp": peer},
+            )
+            copy.start()
+            page_copies.append(copy)
+    for kind in range(2):
+        page_in[kind, grp] = page_out[kind, pl.ds(pl.multiple_of(grp * page, page), page), :]
+
+    total = share(0) + tok[0].astype(jnp.float32)
+    for copy in page_copies:
+        copy.wait_recv()
+    for slot in range(groups):
+        source = jnp.int32(0)
+        for at in range(groups):
+            source = jnp.where(page_table[at * n_row + row, grp] == slot, at, source)
+        page_keys[0, 0, slot] = page_in[0, source]
+        page_values[0, 0, slot] = page_in[1, source]
+    for step in range(1, n_col):
+        mix_copies[step].wait_recv()
+        total = total + incoming[step].astype(jnp.float32)
+    hidden[0] = jnp.where(live, total, 0.0).astype(jnp.bfloat16)
+    for copy in token_copies[1:] + key_copies[1:] + value_copies[1:] + page_copies + mix_copies[1:]:
+        copy.wait_send()
+
+
+def fused(
+    tokens,
+    w_query,
+    w_key,
+    w_value,
+    w_out,
+    diff_lambda,
+    prefix_keys,
+    prefix_values,
+    new_len,
+    prefix_len,
+    holder,
+    page_table,
+):
+    n_col, n_row, groups = lax.axis_size("col"), lax.axis_size("row"), lax.axis_size("grp")
+    slots, cols = tokens.shape[1:]
+    depth, wide = w_query.shape
+    block = prefix_keys.shape[2]
+    page = slots // groups
+    maps = wide // DK
+    scalars = pl.BlockSpec(memory_space=pltpu.SMEM)
+    remains = pl.BlockSpec(memory_space=pl.ANY)
+    whole = pl.BlockSpec(memory_space=pltpu.VMEM)
+    half, full = jnp.bfloat16, jnp.float32
+    return pl.pallas_call(
+        functools.partial(kernel, n_col, n_row),
+        out_shape=(
+            jax.ShapeDtypeStruct((1, slots, cols), half),
+            jax.ShapeDtypeStruct((1, 1, groups, page, wide), half),
+            jax.ShapeDtypeStruct((1, 1, groups, page, wide), half),
+        ),
+        in_specs=[scalars] * 5 + [remains] * 7,
+        out_specs=(whole, whole, whole),
+        scratch_shapes=[
+            pltpu.VMEM((n_col, slots, cols), half),
+            pltpu.VMEM((3, depth, wide), half),
+            pltpu.VMEM(w_out.shape, half),
+            pltpu.VMEM((groups + 1, block, wide), half),
+            pltpu.VMEM((groups + 1, block, wide), half),
+            pltpu.VMEM((3, slots, wide), full),
+            pltpu.VMEM((slots, wide), half),
+            pltpu.VMEM((maps, slots, DV), full),
+            pltpu.VMEM((maps, slots, 1), full),
+            pltpu.VMEM((maps, slots, 1), full),
+            pltpu.VMEM((slots, wide), half),
+            pltpu.VMEM((n_col, slots, cols), half),
+            pltpu.VMEM((n_col, slots, cols), half),
+            pltpu.VMEM((2, slots, wide), half),
+            pltpu.VMEM((2, groups, page, wide), half),
+            pltpu.SemaphoreType.DMA((7,)),
+            pltpu.SemaphoreType.DMA((n_col,)),
+            pltpu.SemaphoreType.DMA((n_col,)),
+            pltpu.SemaphoreType.DMA((2, groups)),
+            pltpu.SemaphoreType.DMA((2, groups)),
+            pltpu.SemaphoreType.DMA((2, groups)),
+            pltpu.SemaphoreType.DMA((2, groups)),
+            pltpu.SemaphoreType.DMA((n_col,)),
+            pltpu.SemaphoreType.DMA((n_col,)),
+        ],
+        compiler_params=pltpu.CompilerParams(
+            collective_id=0, has_side_effects=True, vmem_limit_bytes=48 << 20
+        ),
+    )(
+        new_len,
+        prefix_len,
+        holder,
+        page_table,
+        diff_lambda,
+        tokens,
+        w_query,
+        w_key,
+        w_value,
+        w_out,
+        prefix_keys,
+        prefix_values,
     )
 
 
@@ -52,6 +385,21 @@
     holder,
     page_table,
 ):
+    if fits_kernel(w_query, prefix_keys):
+        return fused(
+            tokens,
+            w_query,
+            w_key,
+            w_value,
+            w_out,
+            diff_lambda,
+            prefix_keys,
+            prefix_values,
+            new_len,
+            prefix_len,
+            holder,
+            page_table,
+        )
     groups = lax.axis_size("grp")
     row_count = lax.axis_size("row")
     grp_index = lax.axis_index("grp")

time: 139 us -> 73.6 us (0.53)
  the two profiles are of different devices: /device:TPU:0 before, /device:TPU:26 now
where the time goes in v1:
time: 73.6 us; the launch traced here: 73.3 us
  Pallas kernels  62.2 us (85%)
  local copies, waits for them, and re-layouts  9.16 us (12%)
  between operations  1.94 us (3%)
    pallas_call x1, Pallas kernels, fused(): pl.pallas_call(functools.partial(kernel, n_col, n_row), out_shape=(jax.Sh...  62.2 us
    unnamed x16, local copies, waits for them, and re-layouts  9.16 us

profile of v1, /device:TPU:26, one launch (start us, length us, event | category | flops | bytes accessed | tf_op | source)
XLA Modules:
  0.0 73.3 jit_solution(9536863218085016683)
XLA Ops:
  1.9 0.8 %copy.15.page_table = s32[8,4]{1,0:T(8,128)S(1)} copy(s32[8,4]{0,1:T(4,128)} %param.23) | data formatting | bytes 256 | tf_op args[11]
  2.7 0.0 copy-start
  2.7 1.6 %copy-done = bf16[2048,512]{1,0:T(8,128)(2,1)S(1)} copy-done((bf16[2048,512]{1,0:T(8,128)(2,1)S(1)}, bf16[2048,512]{1,0:T(8,128)(2,1)}, u32[]{:S(2)}) %copy-start) | copy-done | bytes 2097176
  4.3 0.0 copy-start.1
  4.3 1.2 %copy-done.1 = bf16[1,4,256,512]{3,2,1,0:T(8,128)(2,1)S(1)} copy-done((bf16[1,4,256,512]{3,2,1,0:T(8,128)(2,1)S(1)}, bf16[1,4,256,512]{3,2,1,0:T(8,128)(2,1)}, u32[]{:S(2)}) %copy-start.1) | copy-done | bytes 1048600
  5.5 0.0 copy-start.2
  5.5 1.2 %copy-done.2 = bf16[1,4,256,512]{3,2,1,0:T(8,128)(2,1)S(1)} copy-done((bf16[1,4,256,512]{3,2,1,0:T(8,128)(2,1)S(1)}, bf16[1,4,256,512]{3,2,1,0:T(8,128)(2,1)}, u32[]{:S(2)}) %copy-start.2) | copy-done | bytes 1048600
  6.7 0.0 copy-start.3
  6.7 0.9 %copy-done.3 = bf16[1,256,512]{2,1,0:T(8,128)(2,1)S(1)} copy-done((bf16[1,256,512]{2,1,0:T(8,128)(2,1)S(1)}, bf16[1,256,512]{2,1,0:T(8,128)(2,1)}, u32[]{:S(2)}) %copy-start.3) | copy-done | bytes 262168
  7.7 0.0 copy-start.4
  7.7 0.7 copy-done.4
  8.3 0.0 copy-start.5
  8.3 0.7 copy-done.5
  9.0 62.2 %shard_map.139 = (bf16[1,256,512]{2,1,0:T(8,128)(2,1)S(1)}, bf16[1,1,4,64,512]{4,3,2,1,0:T(8,128)(2,1)S(1)}, bf16[1,1,4,64,512]{4,3,2,1,0:T(8,128)(2,1)S(1)}) custom-call(s32[1]{0:T(128)S(6)} %copy.19.new_len, s32[1]{0:T(128)S(6)} %copy.20.prefix_len, s32[1,4]{1,0:T(1,128)S(1)} %copy-done.4, s32[8,4]{1,0:T(8,128)S(1)} %copy.15.page_table, f32[8]{0:T(128)S(1)} %copy-done.5, ...), custom_call_target="tpu_custom_call" | custom-call | tf_op jit(solution)/shard_map/pallas_call | solution.py:320
  71.2 0.7 copy.21
  71.9 0.7 copy.22
  72.6 0.7 copy.23
Async XLA Ops:
  2.7 1.6 %copy-start = (bf16[2048,512]{1,0:T(8,128)(2,1)S(1)}, bf16[2048,512]{1,0:T(8,128)(2,1)}, u32[]{:S(2)}) copy-start(bf16[2048,512]{1,0:T(8,128)(2,1)} %w_query.1) | copy-start | bytes 6291460
  4.3 1.2 %copy-start.1 = (bf16[1,4,256,512]{3,2,1,0:T(8,128)(2,1)S(1)}, bf16[1,4,256,512]{3,2,1,0:T(8,128)(2,1)}, u32[]{:S(2)}) copy-start(bf16[1,4,256,512]{3,2,1,0:T(8,128)(2,1)} %prefix_keys.1) | copy-start | bytes 3145732
  5.5 1.2 %copy-start.2 = (bf16[1,4,256,512]{3,2,1,0:T(8,128)(2,1)S(1)}, bf16[1,4,256,512]{3,2,1,0:T(8,128)(2,1)}, u32[]{:S(2)}) copy-start(bf16[1,4,256,512]{3,2,1,0:T(8,128)(2,1)} %prefix_values.1) | copy-start | bytes 3145732
  6.7 0.9 %copy-start.3 = (bf16[1,256,512]{2,1,0:T(8,128)(2,1)S(1)}, bf16[1,256,512]{2,1,0:T(8,128)(2,1)}, u32[]{:S(2)}) copy-start(bf16[1,256,512]{2,1,0:T(8,128)(2,1)} %tokens.1) | copy-start | bytes 786436
  7.7 0.7 copy-start.4
  8.3 0.7 copy-start.5

commit v2 on v1

--- a/solution.py
+++ b/solution.py
@@ -194,70 +194,87 @@
     key_at = lax.broadcasted_iota(jnp.int32, (slots, block), 1)
     query_at = lax.broadcasted_iota(jnp.int32, (slots, block), 0)
 
-    def attend(index, allowed, first):
-        def one_head(head):
-            value = vbuf[index, :, head * DV : (head + 1) * DV]
-            for which in range(2):
-                at = head * 2 + which
-                scores = lax.dot_general(
-                    queries[:, at * DK : (at + 1) * DK],
-                    kbuf[index, :, at * DK : (at + 1) * DK],
-                    (((1,), (1,)), ((), ())),
-                    preferred_element_type=jnp.float32,
-                )
-                scores = jnp.where(allowed, scores * scale, MASKED)
-                highest = jnp.max(scores, axis=1, keepdims=True)
-                if not first:
-                    before = top[at]
-                    highest = jnp.maximum(before, highest)
-                weight = jnp.exp2(scores - highest)
-                total = jnp.sum(weight, axis=1, keepdims=True)
-                mixed = jnp.dot(weight.astype(jnp.bfloat16), value, preferred_element_type=jnp.float32)
-                if not first:
-                    decay = jnp.exp2(before - highest)
-                    total = total + low[at] * decay
-                    mixed = mixed + acc[at] * decay
-                top[at] = highest
-                low[at] = total
-                acc[at] = mixed
-
-        for head in range(heads):
-            one_head(head)
-
-    attend(groups, key_at <= query_at, True)
-    for step in range(groups):
-        if step:
-            key_copies[step].wait_recv()
-            value_copies[step].wait_recv()
-        else:
-            copies[4].wait()
-            copies[5].wait()
+    every = pl.ds(0, slots)
+    parts = 2
+    tall = slots // parts
+    ranges = [pl.ds(part * tall, tall) for part in range(parts)]
+
+    def attend(index, allowed, first, rows):
+        for at in range(2 * heads):
+            head = at // 2
+            scores = lax.dot_general(
+                queries[rows, at * DK : (at + 1) * DK],
+                kbuf[index, :, at * DK : (at + 1) * DK],
+                (((1,), (1,)), ((), ())),
+                preferred_element_type=jnp.float32,
+            )
+            scores = jnp.where(allowed, scores * scale, MASKED)
+            highest = jnp.max(scores, axis=1, keepdims=True)
+            if not first:
+                before = top[at, rows]
+                highest = jnp.maximum(before, highest)
+            weight = jnp.exp2(scores - highest)
+            total = jnp.sum(weight, axis=1, keepdims=True)
+            mixed = jnp.dot(
+                weight.astype(jnp.bfloat16),
+                vbuf[index, :, head * DV : (head + 1) * DV],
+                preferred_element_type=jnp.float32,
+            )
+            if not first:
+                decay = jnp.exp2(before - highest)
+                total = total + low[at, rows] * decay
+                mixed = mixed + acc[at, rows] * decay
+            top[at, rows] = highest
+            low[at, rows] = total
+            acc[at, rows] = mixed
+
+    def share(step, rows):
+        first = pl.multiple_of(ahead(step) * cols, cols)
+        return jnp.dot(attended[rows, :], w_last[:, pl.ds(first, cols)], preferred_element_type=jnp.float32)
+
+    def valid(step):
         source = peers[step] if step else grp
         place = jnp.int32(0)
         for at in range(groups):
             place = jnp.where(holder[0, at] == source, at, place)
-        attend(step, key_at < prefix_len[0] - place * block, False)
-
-    for head in range(heads):
-        zero, one = 2 * head, 2 * head + 1
-        differ = acc[zero] / low[zero] - diff_lambda[col * heads + head] * (acc[one] / low[one])
-        normed = OUT_SCALE * differ * lax.rsqrt(jnp.mean(differ * differ, axis=1, keepdims=True) + EPS_HEAD)
-        attended[:, head * DV : (head + 1) * DV] = normed.astype(jnp.bfloat16)
-
+        return prefix_len[0] - place * block
+
+    attend(groups, key_at <= query_at, True, every)
+    copies[4].wait()
+    copies[5].wait()
+    attend(0, key_at < valid(0), False, every)
+    for step in range(1, groups - 1):
+        key_copies[step].wait_recv()
+        value_copies[step].wait_recv()
+        attend(step, key_at < valid(step), False, every)
+    last = groups - 1
+    key_copies[last].wait_recv()
+    value_copies[last].wait_recv()
     copies[6].wait()
-
-    def share(step):
-        first = pl.multiple_of(ahead(step) * cols, cols)
-        return jnp.dot(attended[...], w_last[:, pl.ds(first, cols)], preferred_element_type=jnp.float32)
-
-    mix_copies = [None]
-    for step in range(1, n_col):
-        outgoing[step] = share(step).astype(jnp.bfloat16)
-        copy = remote(
-            outgoing.at[step], incoming.at[step], mix_send.at[step], mix_recv.at[step], {"col": ahead(step)}
-        )
-        copy.start()
-        mix_copies.append(copy)
+    key_in_part = lax.broadcasted_iota(jnp.int32, (tall, block), 1)
+
+    mix_copies = []
+    for part in range(parts):
+        rows = ranges[part]
+        attend(last, key_in_part < valid(last), False, rows)
+        for head in range(heads):
+            zero, one = 2 * head, 2 * head + 1
+            differ = acc[zero, rows] * (1.0 / low[zero, rows]) - acc[one, rows] * (
+                diff_lambda[col * heads + head] / low[one, rows]
+            )
+            normed = OUT_SCALE * differ * lax.rsqrt(jnp.mean(differ * differ, axis=1, keepdims=True) + EPS_HEAD)
+            attended[rows, head * DV : (head + 1) * DV] = normed.astype(jnp.bfloat16)
+        for step in range(n_col - 1, 0, -1):
+            outgoing[step, rows] = share(step, rows).astype(jnp.bfloat16)
+            copy = remote(
+                outgoing.at[step, rows],
+                incoming.at[step, rows],
+                mix_send.at[step, part],
+                mix_recv.at[step, part],
+                {"col": ahead(step)},
+            )
+            copy.start()
+            mix_copies.append((part, step, copy))
 
     page_copies = []
     for step in range(1, groups):
@@ -276,20 +293,24 @@
     for kind in range(2):
         page_in[kind, grp] = page_out[kind, pl.ds(pl.multiple_of(grp * page, page), page), :]
 
-    total = share(0) + tok[0].astype(jnp.float32)
     for copy in page_copies:
         copy.wait_recv()
     for slot in range(groups):
         source = jnp.int32(0)
         for at in range(groups):
-            source = jnp.where(page_table[at * n_row + row, grp] == slot, at, source)
+            source = jnp.where(page_table[grp, at * n_row + row] == slot, at, source)
         page_keys[0, 0, slot] = page_in[0, source]
         page_values[0, 0, slot] = page_in[1, source]
-    for step in range(1, n_col):
-        mix_copies[step].wait_recv()
-        total = total + incoming[step].astype(jnp.float32)
-    hidden[0] = jnp.where(live, total, 0.0).astype(jnp.bfloat16)
-    for copy in token_copies[1:] + key_copies[1:] + value_copies[1:] + page_copies + mix_copies[1:]:
+    for part in range(parts):
+        rows = ranges[part]
+        total = share(0, rows) + tok[0, rows].astype(jnp.float32)
+        for where, step, copy in mix_copies:
+            if where == part:
+                copy.wait_recv()
+                total = total + incoming[step, rows].astype(jnp.float32)
+        at = lax.broadcasted_iota(jnp.int32, (tall, 1), 0) + part * tall
+        hidden[0, rows] = jnp.where(at < new_len[0], total, 0.0).astype(jnp.bfloat16)
+    for copy in token_copies[1:] + key_copies[1:] + value_copies[1:] + page_copies + [copy for _, _, copy in mix_copies]:
         copy.wait_send()
 
 
@@ -314,7 +335,7 @@
     page = slots // groups
     maps = wide // DK
     scalars = pl.BlockSpec(memory_space=pltpu.SMEM)
-    remains = pl.BlockSpec(memory_space=pl.ANY)
+    remains = pl.BlockSpec(memory_space=pltpu.HBM)
     whole = pl.BlockSpec(memory_space=pltpu.VMEM)
     half, full = jnp.bfloat16, jnp.float32
     return pl.pallas_call(
@@ -349,17 +370,17 @@
             pltpu.SemaphoreType.DMA((2, groups)),
             pltpu.SemaphoreType.DMA((2, groups)),
             pltpu.SemaphoreType.DMA((2, groups)),
-            pltpu.SemaphoreType.DMA((n_col,)),
-            pltpu.SemaphoreType.DMA((n_col,)),
+            pltpu.SemaphoreType.DMA((n_col, 2)),
+            pltpu.SemaphoreType.DMA((n_col, 2)),
         ],
         compiler_params=pltpu.CompilerParams(
-            collective_id=0, has_side_effects=True, vmem_limit_bytes=48 << 20
+            collective_id=0, has_side_effects=True, vmem_limit_bytes=56 << 20
         ),
     )(
         new_len,
         prefix_len,
         holder,
-        page_table,
+        page_table.T,
         diff_lambda,
         tokens,
         w_query,

time: 73.6 us -> 66.9 us (0.909)
  the two profiles are of different devices: /device:TPU:26 before, /device:TPU:0 now
where the time goes in v2:
time: 66.9 us; the launch traced here: 66.6 us
  Pallas kernels  59.7 us (89%)
  local copies, waits for them, and re-layouts  5.01 us (7%)
  between operations  1.93 us (3%)
    pallas_call x1, Pallas kernels, fused(): pl.pallas_call(functools.partial(kernel, n_col, n_row), out_shape=(jax.Sh...  59.7 us
    unnamed x3, local copies, waits for them, and re-layouts  5.01 us

profile of v2, /device:TPU:0, one launch (start us, length us, event | category | flops | bytes accessed | tf_op | source)
XLA Modules:
  0.0 66.6 jit_solution(16870818933855090817)
XLA Ops:
  1.9 59.7 %shard_map.139 = (bf16[1,256,512]{2,1,0:T(8,128)(2,1)}, bf16[1,1,4,64,512]{4,3,2,1,0:T(8,128)(2,1)}, bf16[1,1,4,64,512]{4,3,2,1,0:T(8,128)(2,1)}) custom-call(s32[1]{0:T(128)S(6)} %copy.18.new_len, s32[1]{0:T(128)S(6)} %copy.19.prefix_len, s32[1,4]{1,0:T(1,128)} %holder.1, s32[4,8]{1,0:T(4,128)} %bitcast.1, f32[8]{0:T(128)} %diff_lambda.1, ...), custom_call_target="tpu_custom_call" | custom-call | tf_op jit(solution)/shard_map/pallas_call | solution.py:341
  61.6 1.7 %copy.20 = bf16[1,256,512]{2,1,0:T(8,128)(2,1)} copy(bf16[1,256,512]{2,1,0:T(8,128)(2,1)} %get-tuple-element.6) | data formatting | bytes 524288
  63.3 1.7 %copy.21 = bf16[1,1,4,64,512]{4,3,2,1,0:T(8,128)(2,1)} copy(bf16[1,1,4,64,512]{4,3,2,1,0:T(8,128)(2,1)} %get-tuple-element.7) | data formatting | bytes 524288
  65.0 1.7 %copy.22 = bf16[1,1,4,64,512]{4,3,2,1,0:T(8,128)(2,1)} copy(bf16[1,1,4,64,512]{4,3,2,1,0:T(8,128)(2,1)} %get-tuple-element.8) | data formatting | bytes 524288

commit v3 on v2

--- a/solution.py
+++ b/solution.py
@@ -46,7 +46,7 @@
 
 
 def fits_kernel(w_query, prefix_keys):
-    return w_query.shape[1] % (2 * DK) == 0 and lax.axis_size("grp") == 4
+    return w_query.shape[1] % (2 * DK) == 0 and lax.axis_size("grp") == 4 and lax.axis_size("col") == 4
 
 
 def kernel(
@@ -144,8 +144,15 @@
         remote(tokens.at[0], tok.at[step], tok_send.at[step], tok_recv.at[step], {"col": ahead(step)})
         for step in range(1, n_col)
     ]
-    for step in range(1, n_col):
-        token_copies[step].start()
+    inner = jnp.logical_and(col > 0, col < n_col - 1)
+    forward_to = jnp.where(col == 1, 0, 3)
+    forward_slot = jnp.where(col == 1, 1, 3)
+    forward = remote(
+        tok.at[2], tok.at[forward_slot], tok_send.at[0], tok_recv.at[forward_slot], {"col": forward_to}
+    )
+    sends_own = {1: col != 3, 2: col >= 0, 3: col != 0}
+    for step in (2, 1, 3):
+        pl.when(sends_own[step])(token_copies[step].start)
     key_copies, value_copies = [None], [None]
     for step in range(1, groups):
         peer = peers[step]
@@ -166,9 +173,14 @@
     for copy in copies[:4]:
         copy.wait()
     square = jnp.zeros((slots, 1), jnp.float32)
-    for step in range(n_col):
-        if step:
-            token_copies[step].wait_recv()
+    second = jnp.where(col == 0, 3, 1)
+    for turn, step in enumerate((0, 2, second, 4 - second)):
+        if turn:
+            remote(
+                tok.at[step], tok.at[step], tok_send.at[step], tok_recv.at[step], {"col": behind(step)}
+            ).wait_recv()
+        if turn == 1:
+            pl.when(inner)(forward.start)
         shard = tok[step]
         as_float = shard.astype(jnp.float32)
         square = square + jnp.sum(as_float * as_float, axis=1, keepdims=True)
@@ -177,7 +189,7 @@
             part = jnp.dot(
                 shard, weights[which, pl.ds(first, cols), :], preferred_element_type=jnp.float32
             )
-            if step:
+            if turn:
                 part = part + sums[which]
             sums[which] = part
     inv_rms = lax.rsqrt(square / D + EPS_INPUT)
@@ -310,7 +322,10 @@
                 total = total + incoming[step, rows].astype(jnp.float32)
         at = lax.broadcasted_iota(jnp.int32, (tall, 1), 0) + part * tall
         hidden[0, rows] = jnp.where(at < new_len[0], total, 0.0).astype(jnp.bfloat16)
-    for copy in token_copies[1:] + key_copies[1:] + value_copies[1:] + page_copies + [copy for _, _, copy in mix_copies]:
+    for step in range(1, n_col):
+        pl.when(sends_own[step])(token_copies[step].wait_send)
+    pl.when(inner)(forward.wait_send)
+    for copy in key_copies[1:] + value_copies[1:] + page_copies + [copy for _, _, copy in mix_copies]:
         copy.wait_send()
 
 
@@ -374,7 +389,7 @@
             pltpu.SemaphoreType.DMA((n_col, 2)),
         ],
         compiler_params=pltpu.CompilerParams(
-            collective_id=0, has_side_effects=True, vmem_limit_bytes=56 << 20
+            collective_id=0, has_side_effects=True, vmem_limit_bytes=30 << 20
         ),
     )(
         new_len,

time: 66.9 us -> 73.9 us (1.10)
  local copies, waits for them, and re-layouts: 5.01 us -> 13.9 us
  Pallas kernels: 59.7 us -> 57.7 us
    unnamed x3 -> x23, local copies, waits for them, and re-layouts: 5.01 us -> 13.9 us
    pallas_call x1, Pallas kernels: 59.7 us -> 57.7 us  [fused(): pl.pallas_call(functools.partial(kernel, n_col, n_row), out_shape=(jax.Sh...]
where the time goes in v3:
time: 73.9 us; the launch traced here: 73.5 us
  Pallas kernels  57.7 us (78%)
  local copies, waits for them, and re-layouts  13.9 us (19%)
  between operations  1.95 us (3%)
    pallas_call x1, Pallas kernels, fused(): pl.pallas_call(functools.partial(kernel, n_col, n_row), out_shape=(jax.Sh...  57.7 us
    unnamed x23, local copies, waits for them, and re-layouts  13.9 us

profile of v3, /device:TPU:0, one launch (start us, length us, event | category | flops | bytes accessed | tf_op | source)
XLA Modules:
  0.0 73.5 jit_solution(8868744566693125052)
XLA Ops:
  1.9 0.0 copy-start
  1.9 1.6 %copy-done = bf16[2048,512]{1,0:T(8,128)(2,1)S(1)} copy-done((bf16[2048,512]{1,0:T(8,128)(2,1)S(1)}, bf16[2048,512]{1,0:T(8,128)(2,1)}, u32[]{:S(2)}) %copy-start) | copy-done | bytes 2097176
  3.5 0.0 copy-start.1
  3.5 1.6 %copy-done.1 = bf16[2048,512]{1,0:T(8,128)(2,1)S(1)} copy-done((bf16[2048,512]{1,0:T(8,128)(2,1)S(1)}, bf16[2048,512]{1,0:T(8,128)(2,1)}, u32[]{:S(2)}) %copy-start.1) | copy-done | bytes 2097176
  5.1 0.0 copy-start.2
  5.1 1.6 %copy-done.2 = bf16[2048,512]{1,0:T(8,128)(2,1)S(1)} copy-done((bf16[2048,512]{1,0:T(8,128)(2,1)S(1)}, bf16[2048,512]{1,0:T(8,128)(2,1)}, u32[]{:S(2)}) %copy-start.2) | copy-done | bytes 2097176
  6.7 0.0 copy-start.3
  6.7 1.6 %copy-done.3 = bf16[512,2048]{1,0:T(8,128)(2,1)S(1)} copy-done((bf16[512,2048]{1,0:T(8,128)(2,1)S(1)}, bf16[512,2048]{1,0:T(8,128)(2,1)}, u32[]{:S(2)}) %copy-start.3) | copy-done | bytes 2097176
  8.3 0.0 copy-start.4
  8.3 1.2 %copy-done.4 = bf16[1,4,256,512]{3,2,1,0:T(8,128)(2,1)S(1)} copy-done((bf16[1,4,256,512]{3,2,1,0:T(8,128)(2,1)S(1)}, bf16[1,4,256,512]{3,2,1,0:T(8,128)(2,1)}, u32[]{:S(2)}) %copy-start.4) | copy-done | bytes 1048600
  9.5 0.0 copy-start.5
  9.5 1.2 %copy-done.5 = bf16[1,4,256,512]{3,2,1,0:T(8,128)(2,1)S(1)} copy-done((bf16[1,4,256,512]{3,2,1,0:T(8,128)(2,1)S(1)}, bf16[1,4,256,512]{3,2,1,0:T(8,128)(2,1)}, u32[]{:S(2)}) %copy-start.5) | copy-done | bytes 1048600
  10.7 0.0 copy-start.6
  10.7 0.9 %copy-done.6 = bf16[1,256,512]{2,1,0:T(8,128)(2,1)S(1)} copy-done((bf16[1,256,512]{2,1,0:T(8,128)(2,1)S(1)}, bf16[1,256,512]{2,1,0:T(8,128)(2,1)}, u32[]{:S(2)}) %copy-start.6) | copy-done | bytes 262168
  11.7 0.0 copy-start.7
  11.7 0.7 copy-done.7
  12.4 0.0 copy-start.8
  12.4 0.7 copy-done.8
  13.0 0.0 copy-start.9
  13.0 0.7 copy-done.9
  13.7 57.7 %shard_map.139 = (bf16[1,256,512]{2,1,0:T(8,128)(2,1)S(1)}, bf16[1,1,4,64,512]{4,3,2,1,0:T(8,128)(2,1)S(1)}, bf16[1,1,4,64,512]{4,3,2,1,0:T(8,128)(2,1)S(1)}) custom-call(s32[1]{0:T(128)S(6)} %copy.18.new_len, s32[1]{0:T(128)S(6)} %copy.19.prefix_len, s32[1,4]{1,0:T(1,128)S(1)} %copy-done.8, s32[4,8]{1,0:T(4,128)S(1)} %bitcast.1, f32[8]{0:T(128)S(1)} %copy-done.9, ...), custom_call_target="tpu_custom_call" | custom-call | tf_op jit(solution)/shard_map/pallas_call | solution.py:356
  71.4 0.7 copy.20
  72.1 0.7 copy.21
  72.8 0.7 copy.22
Async XLA Ops:
  1.9 1.6 %copy-start = (bf16[2048,512]{1,0:T(8,128)(2,1)S(1)}, bf16[2048,512]{1,0:T(8,128)(2,1)}, u32[]{:S(2)}) copy-start(bf16[2048,512]{1,0:T(8,128)(2,1)} %w_query.1) | copy-start | bytes 6291460
  3.5 1.6 %copy-start.1 = (bf16[2048,512]{1,0:T(8,128)(2,1)S(1)}, bf16[2048,512]{1,0:T(8,128)(2,1)}, u32[]{:S(2)}) copy-start(bf16[2048,512]{1,0:T(8,128)(2,1)} %w_key.1) | copy-start | bytes 6291460
  5.1 1.6 %copy-start.2 = (bf16[2048,512]{1,0:T(8,128)(2,1)S(1)}, bf16[2048,512]{1,0:T(8,128)(2,1)}, u32[]{:S(2)}) copy-start(bf16[2048,512]{1,0:T(8,128)(2,1)} %w_value.1) | copy-start | bytes 6291460
  6.7 1.6 %copy-start.3 = (bf16[512,2048]{1,0:T(8,128)(2,1)S(1)}, bf16[512,2048]{1,0:T(8,128)(2,1)}, u32[]{:S(2)}) copy-start(bf16[512,2048]{1,0:T(8,128)(2,1)} %w_out.1) | copy-start | bytes 6291460
  8.3 1.2 %copy-start.4 = (bf16[1,4,256,512]{3,2,1,0:T(8,128)(2,1)S(1)}, bf16[1,4,256,512]{3,2,1,0:T(8,128)(2,1)}, u32[]{:S(2)}) copy-start(bf16[1,4,256,512]{3,2,1,0:T(8,128)(2,1)} %prefix_keys.1) | copy-start | bytes 3145732
  9.5 1.2 %copy-start.5 = (bf16[1,4,256,512]{3,2,1,0:T(8,128)(2,1)S(1)}, bf16[1,4,256,512]{3,2,1,0:T(8,128)(2,1)}, u32[]{:S(2)}) copy-start(bf16[1,4,256,512]{3,2,1,0:T(8,128)(2,1)} %prefix_values.1) | copy-start | bytes 3145732
  10.7 0.9 %copy-start.6 = (bf16[1,256,512]{2,1,0:T(8,128)(2,1)S(1)}, bf16[1,256,512]{2,1,0:T(8,128)(2,1)}, u32[]{:S(2)}) copy-start(bf16[1,256,512]{2,1,0:T(8,128)(2,1)} %tokens.1) | copy-start | bytes 786436
  11.7 0.7 copy-start.7
  12.4 0.7 copy-start.8
  13.0 0.7 copy-start.9

commit v4 on v3

--- a/solution.py
+++ b/solution.py
@@ -265,6 +265,7 @@
     copies[6].wait()
     key_in_part = lax.broadcasted_iota(jnp.int32, (tall, block), 1)
 
+    crossing = 3 - 2 * lax.rem(col, 2)
     mix_copies = []
     for part in range(parts):
         rows = ranges[part]
@@ -276,7 +277,7 @@
             )
             normed = OUT_SCALE * differ * lax.rsqrt(jnp.mean(differ * differ, axis=1, keepdims=True) + EPS_HEAD)
             attended[rows, head * DV : (head + 1) * DV] = normed.astype(jnp.bfloat16)
-        for step in range(n_col - 1, 0, -1):
+        for step in (2, crossing, 4 - crossing):
             outgoing[step, rows] = share(step, rows).astype(jnp.bfloat16)
             copy = remote(
                 outgoing.at[step, rows],
@@ -389,7 +390,7 @@
             pltpu.SemaphoreType.DMA((n_col, 2)),
         ],
         compiler_params=pltpu.CompilerParams(
-            collective_id=0, has_side_effects=True, vmem_limit_bytes=30 << 20
+            collective_id=0, has_side_effects=True, vmem_limit_bytes=56 << 20
         ),
     )(
         new_len,

time: 73.9 us -> 64.2 us (0.87)
  local copies, waits for them, and re-layouts: 13.9 us -> 5.01 us
    unnamed x23 -> x3, local copies, waits for them, and re-layouts: 13.9 us -> 5.01 us
where the time goes in v4:
time: 64.2 us; the launch traced here: 63.9 us
  Pallas kernels  57 us (89%)
  local copies, waits for them, and re-layouts  5.01 us (8%)
  between operations  1.93 us (3%)
    pallas_call x1, Pallas kernels, fused(): pl.pallas_call(functools.partial(kernel, n_col, n_row), out_shape=(jax.Sh...  57 us
    unnamed x3, local copies, waits for them, and re-layouts  5.01 us

profile of v4, /device:TPU:0, one launch (start us, length us, event | category | flops | bytes accessed | tf_op | source)
XLA Modules:
  0.0 63.9 jit_solution(14578398665598324199)
XLA Ops:
  1.9 57.0 %shard_map.139 = (bf16[1,256,512]{2,1,0:T(8,128)(2,1)}, bf16[1,1,4,64,512]{4,3,2,1,0:T(8,128)(2,1)}, bf16[1,1,4,64,512]{4,3,2,1,0:T(8,128)(2,1)}) custom-call(s32[1]{0:T(128)S(6)} %copy.18.new_len, s32[1]{0:T(128)S(6)} %copy.19.prefix_len, s32[1,4]{1,0:T(1,128)} %holder.1, s32[4,8]{1,0:T(4,128)} %bitcast.1, f32[8]{0:T(128)} %diff_lambda.1, ...), custom_call_target="tpu_custom_call" | custom-call | tf_op jit(solution)/shard_map/pallas_call | solution.py:357
  58.9 1.7 %copy.20 = bf16[1,256,512]{2,1,0:T(8,128)(2,1)} copy(bf16[1,256,512]{2,1,0:T(8,128)(2,1)} %get-tuple-element.6) | data formatting | bytes 524288
  60.6 1.7 %copy.21 = bf16[1,1,4,64,512]{4,3,2,1,0:T(8,128)(2,1)} copy(bf16[1,1,4,64,512]{4,3,2,1,0:T(8,128)(2,1)} %get-tuple-element.7) | data formatting | bytes 524288
  62.3 1.7 %copy.22 = bf16[1,1,4,64,512]{4,3,2,1,0:T(8,128)(2,1)} copy(bf16[1,1,4,64,512]{4,3,2,1,0:T(8,128)(2,1)} %get-tuple-element.8) | data formatting | bytes 524288

commit v5 on v4

--- a/solution.py
+++ b/solution.py
@@ -266,7 +266,29 @@
     key_in_part = lax.broadcasted_iota(jnp.int32, (tall, block), 1)
 
     crossing = 3 - 2 * lax.rem(col, 2)
-    mix_copies = []
+    third = 4 - crossing
+
+    def direct(part, step, slot, target):
+        return remote(
+            outgoing.at[step, ranges[part]],
+            incoming.at[slot, ranges[part]],
+            mix_send.at[step, part],
+            mix_recv.at[slot, part],
+            {"col": target},
+        )
+
+    def middle(part, relays):
+        total = share(2, ranges[part])
+        if relays:
+            direct(part, 2, 0, ahead(2)).wait_recv()
+            total = total + incoming[0, ranges[part]].astype(jnp.float32)
+        outgoing[2, ranges[part]] = total.astype(jnp.bfloat16)
+        direct(part, 2, 2, ahead(2)).start()
+
+    @pl.when(jnp.logical_not(inner))
+    def _():
+        incoming[third] = jnp.zeros((slots, cols), jnp.bfloat16)
+
     for part in range(parts):
         rows = ranges[part]
         attend(last, key_in_part < valid(last), False, rows)
@@ -277,17 +299,15 @@
             )
             normed = OUT_SCALE * differ * lax.rsqrt(jnp.mean(differ * differ, axis=1, keepdims=True) + EPS_HEAD)
             attended[rows, head * DV : (head + 1) * DV] = normed.astype(jnp.bfloat16)
-        for step in (2, crossing, 4 - crossing):
-            outgoing[step, rows] = share(step, rows).astype(jnp.bfloat16)
-            copy = remote(
-                outgoing.at[step, rows],
-                incoming.at[step, rows],
-                mix_send.at[step, part],
-                mix_recv.at[step, part],
-                {"col": ahead(step)},
-            )
-            copy.start()
-            mix_copies.append((part, step, copy))
+        slot = jnp.where(inner, crossing, 0)
+        target = jnp.where(inner, ahead(crossing), jnp.where(col == 0, 1, 2))
+        outgoing[crossing, rows] = share(crossing, rows).astype(jnp.bfloat16)
+        direct(part, crossing, slot, target).start()
+        pl.when(jnp.logical_not(inner))(functools.partial(middle, part, False))
+        outgoing[third, rows] = share(third, rows).astype(jnp.bfloat16)
+        direct(part, third, third, ahead(third)).start()
+    for part in range(parts):
+        pl.when(inner)(functools.partial(middle, part, True))
 
     page_copies = []
     for step in range(1, groups):
@@ -317,16 +337,17 @@
     for part in range(parts):
         rows = ranges[part]
         total = share(0, rows) + tok[0, rows].astype(jnp.float32)
-        for where, step, copy in mix_copies:
-            if where == part:
-                copy.wait_recv()
-                total = total + incoming[step, rows].astype(jnp.float32)
+        pl.when(inner)(direct(part, third, third, ahead(third)).wait_recv)
+        for step in (crossing, 2):
+            direct(part, step, step, ahead(step)).wait_recv()
+        for step in range(1, n_col):
+            total = total + incoming[step, rows].astype(jnp.float32)
         at = lax.broadcasted_iota(jnp.int32, (tall, 1), 0) + part * tall
         hidden[0, rows] = jnp.where(at < new_len[0], total, 0.0).astype(jnp.bfloat16)
     for step in range(1, n_col):
         pl.when(sends_own[step])(token_copies[step].wait_send)
     pl.when(inner)(forward.wait_send)
-    for copy in key_copies[1:] + value_copies[1:] + page_copies + [copy for _, _, copy in mix_copies]:
+    for copy in key_copies[1:] + value_copies[1:] + page_copies + [direct(part, step, step, ahead(step)) for part in range(parts) for step in range(1, n_col)]:
         copy.wait_send()
 
 

time: 64.2 us -> 61.9 us (0.964)
  Pallas kernels: 57 us -> 54.5 us
    pallas_call x1, Pallas kernels: 57 us -> 54.5 us  [fused(): pl.pallas_call(functools.partial(kernel, n_col, n_row), out_shape=(jax.Sh...]
where the time goes in v5:
time: 61.9 us; the launch traced here: 61.4 us
  Pallas kernels  54.5 us (88%)
  local copies, waits for them, and re-layouts  5.01 us (8%)
  between operations  1.93 us (3%)
    pallas_call x1, Pallas kernels, fused(): pl.pallas_call(functools.partial(kernel, n_col, n_row), out_shape=(jax.Sh...  54.5 us
    unnamed x3, local copies, waits for them, and re-layouts  5.01 us

profile of v5, /device:TPU:0, one launch (start us, length us, event | category | flops | bytes accessed | tf_op | source)
XLA Modules:
  0.0 61.4 jit_solution(8862063859001917439)
XLA Ops:
  1.9 54.5 %shard_map.139 = (bf16[1,256,512]{2,1,0:T(8,128)(2,1)}, bf16[1,1,4,64,512]{4,3,2,1,0:T(8,128)(2,1)}, bf16[1,1,4,64,512]{4,3,2,1,0:T(8,128)(2,1)}) custom-call(s32[1]{0:T(128)S(6)} %copy.18.new_len, s32[1]{0:T(128)S(6)} %copy.19.prefix_len, s32[1,4]{1,0:T(1,128)} %holder.1, s32[4,8]{1,0:T(4,128)} %bitcast.1, f32[8]{0:T(128)} %diff_lambda.1, ...), custom_call_target="tpu_custom_call" | custom-call | tf_op jit(solution)/shard_map/pallas_call | solution.py:378
  56.4 1.7 %copy.20 = bf16[1,256,512]{2,1,0:T(8,128)(2,1)} copy(bf16[1,256,512]{2,1,0:T(8,128)(2,1)} %get-tuple-element.6) | data formatting | bytes 524288
  58.1 1.7 %copy.21 = bf16[1,1,4,64,512]{4,3,2,1,0:T(8,128)(2,1)} copy(bf16[1,1,4,64,512]{4,3,2,1,0:T(8,128)(2,1)} %get-tuple-element.7) | data formatting | bytes 524288
  59.7 1.7 %copy.22 = bf16[1,1,4,64,512]{4,3,2,1,0:T(8,128)(2,1)} copy(bf16[1,1,4,64,512]{4,3,2,1,0:T(8,128)(2,1)} %get-tuple-element.8) | data formatting | bytes 524288
